TPU v7x, 128 devices: a whole 4x4x4 slice. The times are simulated.
128 devices in a mesh: row: 8 (over y, z_hi), col: 16 (over z_lo, x, core).
Axes of the slice: x: 4, y: 4, z: 4 (z_hi: 2, z_lo: 2; z = z_hi * 2 + z_lo), core: 2. Of those that a mesh axis runs over, the one named last changes fastest.
Arguments:
- features: float32 [2, 128, 1024, 128], P(None, 'row', 'col'), may hold values from -6 to 6
- cotangent: float32 [2, 128, 1024, 128], P(None, 'row', 'col'), may hold values from -6 to 6
- conv_kernel: float32 [7, 7, 128], P(None, None, ('row', 'col')), may hold values from -0.875 to 0.875
- conv_bias: float32 [128], P(('row', 'col')), may hold values from -3 to 3
- norm_gain: float32 [128], P(('row', 'col')), may hold values from 0.1 to 1.9
- norm_shift: float32 [128], P(('row', 'col')), may hold values from -2 to 2
- w_in: float32 [128, 512], P(None, ('row', 'col')), may hold values from -0.5 to 0.5
- in_bias: float32 [512], P(('row', 'col')), may hold values from -3 to 3
- w_out: float32 [512, 128], P(('row', 'col')), may hold values from -0.25 to 0.25
- out_bias: float32 [128], P(('row', 'col')), may hold values from -3 to 3
- layer_scale: float32 [128], P(('row', 'col')), may hold values from 0.5 to 1.5
Outputs:
- features_grad: float32 [2, 128, 1024, 128], P(None, 'row', 'col')
- kernel_grad: float32 [7, 7, 128], P(None, None, ('row', 'col'))
- conv_bias_grad: float32 [128], P(('row', 'col'))
- gain_grad: float32 [128], P(('row', 'col'))
- shift_grad: float32 [128], P(('row', 'col'))
- w_in_grad: float32 [128, 512], P(None, ('row', 'col'))
- in_bias_grad: float32 [512], P(('row', 'col'))
- w_out_grad: float32 [512, 128], P(('row', 'col'))
- out_bias_grad: float32 [128], P(('row', 'col'))
- scale_grad: float32 [128], P(('row', 'col'))
All inputs are finite; a program needn't handle non-finite values.
Results may differ from a plain program's by a relative error of at most 0.0003.
Values sent between devices are 32-bit elements; how exact they have to be, the bound alone decides.
A program may use at most 64 MiB of HBM per device.

v0:
```python
import math
import jax
import jax.numpy as jnp
from jax import lax
from jax.sharding import PartitionSpec as P

norm_eps = 1e-06
inverse_root_two = 0.7071067811865476
inverse_root_twopi = 0.3989422804014327


def extended(block, sides, width):
    for axis, dim in sides:
        count = lax.axis_size(axis)
        forward = [(i, i + 1) for i in range(count - 1)]
        backward = [(target, source) for source, target in forward]
        low = lax.ppermute(
            lax.slice_in_dim(block, block.shape[dim] - width, None, axis=dim), axis, forward
        )
        high = lax.ppermute(lax.slice_in_dim(block, 0, width, axis=dim), axis, backward)
        block = jnp.concatenate([low, block, high], axis=dim)
    return block


def depthwise(field, kernel):
    return lax.conv_general_dilated(
        field,
        kernel[:, :, None, :],
        (1, 1),
        "VALID",
        dimension_numbers=("NHWC", "HWIO", "NHWC"),
        feature_group_count=field.shape[-1],
        precision=lax.Precision.HIGHEST,
    )


def cell_total(block):
    return jnp.sum(block, axis=(0, 1, 2))


def mixing_back(
    conv_out,
    cot_field,
    gain_all,
    shift_all,
    input_all,
    inbias_all,
    output_all,
    outbias_all,
    scale_all,
):
    highest = lax.Precision.HIGHEST
    mean = jnp.mean(conv_out, -1, keepdims=True)
    centred = conv_out - mean
    variance = jnp.mean(centred * centred, -1, keepdims=True)
    inverse = lax.rsqrt(variance + norm_eps)
    normed = centred * inverse
    lin = normed * gain_all + shift_all
    act = jnp.einsum("bhwc,ck->bhwk", lin, input_all, precision=highest) + inbias_all
    hidden = 0.5 * act * (1.0 + lax.erf(act * inverse_root_two))
    branch = jnp.einsum("bhwk,kc->bhwc", hidden, output_all, precision=highest) + outbias_all
    d_branch = cot_field * scale_all
    d_hidden = jnp.einsum("bhwc,kc->bhwk", d_branch, output_all, precision=highest)
    slope = (
        0.5 * (1.0 + lax.erf(act * inverse_root_two))
        + act * jnp.exp(-0.5 * act * act) * inverse_root_twopi
    )
    d_act = d_hidden * slope
    d_lin = jnp.einsum("bhwk,ck->bhwc", d_act, input_all, precision=highest)
    d_norm = d_lin * gain_all
    d_conv = inverse * (
        d_norm
        - jnp.mean(d_norm, -1, keepdims=True)
        - normed * jnp.mean(d_norm * normed, -1, keepdims=True)
    )
    gain_grad = cell_total(d_lin * normed)
    shift_grad = cell_total(d_lin)
    win_grad = jnp.einsum("bhwc,bhwk->ck", lin, d_act, precision=highest)
    inb_grad = cell_total(d_act)
    wout_grad = jnp.einsum("bhwk,bhwc->kc", hidden, d_branch, precision=highest)
    outb_grad = cell_total(d_branch)
    scale_grad = cell_total(cot_field * branch)
    return (d_conv, (gain_grad, shift_grad, win_grad, inb_grad, wout_grad, outb_grad, scale_grad))


def per_device(
    features,
    cotangent,
    conv_kernel,
    conv_bias,
    norm_gain,
    norm_shift,
    w_in,
    in_bias,
    w_out,
    out_bias,
    layer_scale,
):
    gathered = (
        lax.all_gather(conv_kernel, ("row", "col"), axis=2, tiled=True),
        lax.all_gather(conv_bias, ("row", "col"), axis=0, tiled=True),
        lax.all_gather(norm_gain, ("row", "col"), axis=0, tiled=True),
        lax.all_gather(norm_shift, ("row", "col"), axis=0, tiled=True),
        lax.all_gather(w_in, ("row", "col"), axis=1, tiled=True),
        lax.all_gather(in_bias, ("row", "col"), axis=0, tiled=True),
        lax.all_gather(w_out, ("row", "col"), axis=0, tiled=True),
        lax.all_gather(out_bias, ("row", "col"), axis=0, tiled=True),
        lax.all_gather(layer_scale, ("row", "col"), axis=0, tiled=True),
    )
    (
        kernel_all,
        conv_all,
        gain_all,
        shift_all,
        input_all,
        inbias_all,
        output_all,
        outbias_all,
        scale_all,
    ) = gathered
    margin = kernel_all.shape[0] // 2
    source = extended(features, (("row", 1), ("col", 2)), margin)
    conv_out = depthwise(source, kernel_all) + conv_all
    dconv_inner, partials = mixing_back(
        conv_out,
        cotangent,
        gain_all,
        shift_all,
        input_all,
        inbias_all,
        output_all,
        outbias_all,
        scale_all,
    )
    dconv_wide = extended(dconv_inner, (("row", 1), ("col", 2)), margin)
    features_grad = cotangent + depthwise(dconv_wide, kernel_all[::-1, ::-1])
    kernel_part = jax.vjp(lambda weights: depthwise(source, weights), kernel_all)[1](dconv_inner)[0]
    bias_part = jnp.sum(dconv_inner, axis=(0, 1, 2))
    cells = (
        features.shape[0]
        * features.shape[1]
        * features.shape[2]
        * lax.axis_size("row")
        * lax.axis_size("col")
    )
    factor = 1.0 / math.sqrt(cells)
    gain_p, shift_p, win_p, inb_p, wout_p, outb_p, scale_p = partials
    reduced = (
        lax.psum_scatter(kernel_part * factor, ("row", "col"), scatter_dimension=2, tiled=True),
        lax.psum_scatter(bias_part * factor, ("row", "col"), scatter_dimension=0, tiled=True),
        lax.psum_scatter(gain_p * factor, ("row", "col"), scatter_dimension=0, tiled=True),
        lax.psum_scatter(shift_p * factor, ("row", "col"), scatter_dimension=0, tiled=True),
        lax.psum_scatter(win_p * factor, ("row", "col"), scatter_dimension=1, tiled=True),
        lax.psum_scatter(inb_p * factor, ("row", "col"), scatter_dimension=0, tiled=True),
        lax.psum_scatter(wout_p * factor, ("row", "col"), scatter_dimension=0, tiled=True),
        lax.psum_scatter(outb_p * factor, ("row", "col"), scatter_dimension=0, tiled=True),
        lax.psum_scatter(scale_p * factor, ("row", "col"), scatter_dimension=0, tiled=True),
    )
    (
        kernel_grad,
        bias_grad,
        gain_grad,
        shift_grad,
        win_grad,
        inb_grad,
        wout_grad,
        outb_grad,
        scale_grad,
    ) = reduced
    return (
        features_grad,
        kernel_grad,
        bias_grad,
        gain_grad,
        shift_grad,
        win_grad,
        inb_grad,
        wout_grad,
        outb_grad,
        scale_grad,
    )


def solution(mesh):
    in_specs = (
        P(None, "row", "col", None),
        P(None, "row", "col", None),
        P(None, None, ("row", "col")),
        P(("row", "col")),
        P(("row", "col")),
        P(("row", "col")),
        P(None, ("row", "col")),
        P(("row", "col")),
        P(("row", "col"), None),
        P(("row", "col")),
        P(("row", "col")),
    )
    out_specs = (
        P(None, "row", "col", None),
        P(None, None, ("row", "col")),
        P(("row", "col")),
        P(("row", "col")),
        P(("row", "col")),
        P(None, ("row", "col")),
        P(("row", "col")),
        P(("row", "col"), None),
        P(("row", "col")),
        P(("row", "col")),
    )
    return jax.shard_map(
        per_device, mesh=mesh, in_specs=in_specs, out_specs=out_specs, check_vma=False
    )
```

profile of v0, /device:TPU:1, one launch (start us, length us, event | category | flops | bytes accessed | tf_op | source)
XLA Modules:
  0.0 425.7 jit_solution(4927064167426286075)
XLA Ops:
  9.2 7.0 %collective-permute-start = (f32[2,3,64,128]{3,0,2,1:T(2,128)}, f32[2,3,64,128]{3,0,2,1:T(2,128)}, u32[]{:S(2)}, u32[]{:S(2)}) collective-permute-start(f32[2,3,64,128]{3,0,2,1:T(2,128)} %copy.127), channel_id=1, source_target_pairs={{0,16},{16,32},{32,48},{48,64},{64,80},{80,96},{96,112},{1,17},{17... | collective-permute-start | bytes 589832 | tf_op jit(solution)/shard_map/ppermute | solution.py:17
  18.3 38.5 %all-gather.1 = f32[128,4,128]{2,1,0:T(4,128)S(1)} all-gather(f32[1,4,128]{2,1,0:T(4,128)} %bitcast.98), channel_id=1, replica_groups=mesh['row'=8,'col'=16] {'row','col'}, dimensions={0}, use_global_device_ids=true | all-gather | bytes 264192 | tf_op jit(solution)/shard_map/all_gather | solution.py:104
  60.8 33.9 %all_gather.27 = f32[7,7,128]{1,0,2:T(8,128)S(1)} all-gather(f32[7,7,1]{1,0,2:T(8,128)S(1)} %copy.73), channel_id=1, replica_groups=mesh['row'=8,'col'=16] {'row','col'}, dimensions={2}, use_global_device_ids=true | all-gather | bytes 25284 | tf_op jit(solution)/shard_map/all_gather | solution.py:100
  97.0 63.9 %all-reduce.16 = (f32[128]{0:T(128)S(1)}, f32[128]{0:T(128)S(1)}, f32[128]{0:T(128)}, f32[512]{0:T(512)}, f32[128]{0:T(128)S(1)}, /*index=5*/f32[128]{0:T(128)}) all-reduce(f32[128]{0:T(128)S(1)} %dynamic-update-slice.3, f32[128]{0:T(128)S(1)} %dynamic-update-slice.2, ...), channel_id=1, replica_groups=mesh['row'=8,'col'=16] {'row','col'}, use_global_device_ids=true, to_apply=%add.3 | all-reduce | flops 1152 | bytes 9216
  164.0 1.9 collective-permute-start.2
  165.9 2.4 collective-permute-start.3
  168.3 37.6 %all-gather = f32[128,4,128]{2,1,0:T(4,128)S(1)} all-gather(f32[1,4,128]{2,1,0:T(4,128)S(1)} %bitcast.99), channel_id=1, replica_groups=mesh['row'=8,'col'=16] {'row','col'}, dimensions={0}, use_global_device_ids=true | all-gather | bytes 264192 | tf_op jit(solution)/shard_map/all_gather | solution.py:106
  208.1 5.9 %fusion.56 = (f32[16,16,9]{1,2,0:T(8,128)S(1)}, f32[16,16,9,128]{3,1,2,0:T(8,128)S(1)}) fusion(f32[128]{0:T(128)S(1)} %copy-done.15, f32[7,7,1,128]{3,2,1,0:T(1,128)S(1)} %copy-done.7, f32[22,2,7,6,128]{4,2,1,3,0:T(8,128)S(1)} %slice.41, f32[22,2,8,9,128]{4,2,1,3,0:T(8,128)S(1)} %copy.72, pred[16,9]{0,1:T(8,128)(4,1)S(1)} %copy-done.16), kind=kOutput, calls=%fused_computation.87 | convolution fusion | flops 176318208 | bytes 3782800 | tf_op jit(solution)/shard_map/conv_general_dilated | solution.py:26
  215.6 3.6 fusion.34
  219.2 8.0 %fusion.30 = f32[512,128]{1,0:T(8,128)} fusion(f32[2,16,64,512]{3,2,1,0:T(8,128)S(1)} %fusion.34, f32[512]{0:T(512)S(1)} %copy-done.12, f32[2,16,64,128]{3,2,1,0:T(8,128)S(1)} %copy-done.1, f32[128]{0:T(128)S(1)} %copy-done.10), kind=kOutput, calls=%fused_computation.33 | convolution fusion | flops 1616183296 | bytes 5507584 | tf_op jit(solution)/shard_map/bhwk,bhwc->kc/dot_general | solution.py:80
  227.3 5.2 %fusion.57 = (f32[512]{0:T(512)S(1)}, f32[2,16,64,512]{3,2,1,0:T(8,128)S(1)}) fusion(f32[2,16,64,512]{3,2,1,0:T(8,128)S(1)} %fusion.34, f32[512]{0:T(512)S(1)} %copy-done.12, f32[512,128,1,1]{1,0,3,2:T(8,128)S(1)} %bitcast.96, f32[2,16,64,128]{3,2,1,0:T(8,128)S(1)} %copy-done.1, f32[128]{0:T(128)S(1)} %copy-done.10), kind=kOutput, calls=%fused_computation.88 | convolution fusion | flops 1622408704 | bytes 9703936 | tf_op jit(solution)/shard_map/bhwc,kc->bhwk/dot_general | solution.py:63
  232.4 2.0 copy-done
  234.4 8.2 %fusion.28 = f32[128,512]{0,1:T(8,128)} fusion(f32[2,16,64,512]{3,2,1,0:T(8,128)S(1)} %get-tuple-element.83, f32[128]{0:T(128)S(1)} %get-tuple-element.61, f32[128]{0:T(128)S(1)} %get-tuple-element.62, f32[16,2,64,128]{3,0,2,1:T(8,128)S(1)} %slice.42, f32[2,16,64]{2,1,0:T(8,128)S(1)} %add_rsqrt_fusion, f32[2,16,64]{2,1,0:T(8,128)S(1)} %copy.79), kind=kOutput, calls=%fused_computation.31 | convolution fusion | flops 1611726848 | bytes 5522432 | tf_op jit(solution)/shard_map/bhwc,bhwk->ck/dot_general | solution.py:78
  242.7 5.7 %multiply_reduce_fusion = (f32[128]{0:T(128)S(1)}, f32[2,16,64]{2,1,0:T(8,128)S(1)}, f32[2,16,64]{2,1,0:T(8,128)S(1)}, f32[128]{0:T(128)S(1)}, f32[2,16,64,128]{3,2,1,0:T(8,128)S(1)}) fusion(f32[2,16,64]{2,1,0:T(8,128)S(1)} %add_rsqrt_fusion, f32[2,16,64]{2,1,0:T(8,128)S(1)} %copy.79, f32[16,2,64,128]{3,0,2,1:T(8,128)S(1)} %slice.42, ...), kind=kOutput, calls=%fused_computation.40 | convolution fusion | flops 1612967680 | bytes 6587904 | tf_op jit(solution)/shard_map/bhwk,ck->bhwc/dot_general | solution.py:69
  248.4 4.1 fusion.27
  252.5 1.8 fusion.52
  254.3 3.1 collective-permute-start.4
  257.5 1.7 collective-permute-start.5
  259.2 21.3 %convolution_multiply_fusion = f32[7,7,1,128]{3,2,1,0:T(1,128)S(1)} fusion(f32[2,16,64,128]{3,2,1,0:T(8,128)S(1)} %get-tuple-element.70, f32[2,22,3,128]{3,0,2,1:T(2,128)} %copy-done.6, f32[2,22,64,128]{3,0,2,1:T(2,128)} %copy-done.4, f32[2,22,3,128]{3,0,2,1:T(2,128)S(1)} %collective-permute-done.2), kind=kOutput, calls=%fused_computation.34 | convolution fusion | flops 154935424 | bytes 2650624 | tf_op jit(solution)/shard_map/transpose(jvp())/conv_general_dilated | solution.py:26
  280.8 70.8 %all-reduce.15 = (f32[7,7,128]{1,0,2:T(8,128)}, f32[128]{0:T(128)S(1)}, f32[128]{0:T(128)S(1)}, f32[128]{0:T(128)S(1)}, f32[512]{0:T(512)S(1)}, /*index=5*/f32[128]{0:T(128)S(1)}, f32[128]{0:T(128)S(1)}) all-reduce(f32[7,7,128]{1,0,2:T(8,128)S(1)} %bitcast.94, ...), channel_id=2, replica_groups=mesh['row'=8,'col'=16] {'row','col'}, use_global_device_ids=true, to_apply=%region_4.0.clone | all-reduce | flops 7424 | bytes 59392
  356.5 2.4 collective-permute-start.6
  358.9 2.1 collective-permute-start.7
  361.0 44.3 %all-reduce.20.cloned.1.call-done = (f32[128,512]{0,1:T(8,128)}, f32[512,128]{1,0:T(8,128)}) async-done(((f32[128,512]{0,1:T(8,128)}, f32[512,128]{1,0:T(8,128)}), (f32[128,512]{0,1:T(8,128)}, f32[512,128]{1,0:T(8,128)})) %all-reduce.20.cloned.1.call-update) | async-done | bytes 524304
  410.8 5.4 %fusion.18 = f32[16,16,9,128]{3,1,2,0:T(8,128)S(1)} fusion(f32[7,7,1,128]{3,2,1,0:T(1,128)S(1)} %copy.82, f32[22,2,8,15,128]{4,1,3,2,0:T(2,128)S(1)} %fusion.5, pred[16,9]{0,1:T(8,128)(4,1)S(1)} %copy-done.17), kind=kOutput, calls=%fused_computation.26 | convolution fusion | flops 173703168 | bytes 3908240 | tf_op jit(solution)/shard_map/conv_general_dilated | solution.py:26
  (109 shorter events, 26.5 us)
Async XLA Ops:
  7.2 89.5 %copy-start.13 = (f32[4]{0:T(128)S(1)}, f32[4]{0:T(128)}, u32[]{:S(2)}) copy-start(f32[4]{0:T(128)} %param.18) | copy-start | bytes 52
  7.2 153.6 %copy-start.1 = (f32[2,16,64,128]{3,2,1,0:T(8,128)S(1)}, f32[2,16,64,128]{3,2,1,0:T(8,128)}, u32[]{:S(2)}) copy-start(f32[2,16,64,128]{3,2,1,0:T(8,128)} %param.12) | copy-start | bytes 3145732
  7.2 398.1 %all-reduce.20.cloned.1.call-start = ((), (), s32[]{:S(2)}) async-start(), calls=%async_computation | async-start | bytes 1048576
  8.4 153.7 %copy-start.5 = (f32[2,16,64,128]{3,2,1,0:T(8,128)S(1)}, f32[2,16,64,128]{3,2,1,0:T(8,128)}, u32[]{:S(2)}) copy-start(f32[2,16,64,128]{3,2,1,0:T(8,128)} %param.11) | copy-start | bytes 3145732
  9.2 151.9 %collective-permute-start = (f32[2,3,64,128]{3,0,2,1:T(2,128)}, f32[2,3,64,128]{3,0,2,1:T(2,128)}, u32[]{:S(2)}, u32[]{:S(2)}) collective-permute-start(f32[2,3,64,128]{3,0,2,1:T(2,128)} %copy.127), channel_id=1, source_target_pairs={{0,16},{16,32},{32,48},{48,64},{64,80},{80,96},{96,112},{1,17},{17... | collective-permute-start | bytes 589832 | tf_op jit(solution)/shard_map/ppermute | solution.py:17
  17.0 145.9 %collective-permute-start.1 = (f32[2,3,64,128]{3,0,2,1:T(2,128)}, f32[2,3,64,128]{3,0,2,1:T(2,128)}, u32[]{:S(2)}, u32[]{:S(2)}) collective-permute-start(f32[2,3,64,128]{3,0,2,1:T(2,128)} %copy.128), channel_id=1, source_target_pairs={{16,0},{32,16},{48,32},{64,48},{80,64},{96,80},{112,96},{17,1},{33... | collective-permute-start | bytes 589832 | tf_op jit(solution)/shard_map/ppermute | solution.py:20
  95.2 73.2 %copy-start.8 = (f32[4,128]{1,0:T(4,128)S(1)}, f32[4,128]{1,0:T(4,128)}, u32[]{:S(2)}) copy-start(f32[4,128]{1,0:T(4,128)} %param.19) | copy-start | bytes 6148
  160.8 7.5 %copy-start.9 = (f32[128]{0:T(128)}, f32[128]{0:T(128)S(1)}, u32[]{:S(2)}) copy-start(f32[128]{0:T(128)S(1)} %get-tuple-element.65) | copy-start | bytes 1540
  163.9 43.4 %copy-start.4 = (f32[2,22,64,128]{3,0,2,1:T(2,128)}, f32[2,22,64,128]{3,0,2,1:T(2,128)S(1)}, u32[]{:S(2)}) copy-start(f32[2,22,64,128]{3,0,2,1:T(2,128)S(1)} %constant_dynamic-update-slice_fusion) | copy-start | bytes 4325380
  164.0 42.0 %collective-permute-start.2 = (f32[2,22,3,128]{3,0,2,1:T(2,128)S(1)}, f32[2,22,3,128]{3,0,2,1:T(2,128)S(1)}, u32[]{:S(2)}, u32[]{:S(2)}) collective-permute-start(f32[2,22,3,128]{3,0,2,1:T(2,128)S(1)} %get-tuple-element.73), channel_id=1, source_target_pairs={{0,1},{1,2},{2,3},{3,4},{4,5},{5,6},{6,7},{7,8},{8,9},{9,10},{10,1... | collective-permute-start | bytes 202760 | tf_op jit(solution)/shard_map/ppermute | solution.py:17
  165.9 40.1 %collective-permute-start.3 = (f32[2,22,3,128]{3,0,2,1:T(2,128)S(1)}, f32[2,22,3,128]{3,0,2,1:T(2,128)S(1)}, u32[]{:S(2)}, u32[]{:S(2)}) collective-permute-start(f32[2,22,3,128]{3,0,2,1:T(2,128)S(1)} %get-tuple-element.74), channel_id=1, source_target_pairs={{1,0},{2,1},{3,2},{4,3},{5,4},{6,5},{7,6},{8,7},{9,8},{10,9},{11,1... | collective-permute-start | bytes 202760 | tf_op jit(solution)/shard_map/ppermute | solution.py:20
  206.0 1.6 copy-start.6
  215.5 3.7 copy-start.10
  215.5 3.7 copy-start.12
  219.2 8.1 %copy-start.2 = (f32[2,16,64,512]{3,2,1,0:T(8,128)}, f32[2,16,64,512]{3,2,1,0:T(8,128)S(1)}, u32[]{:S(2)}) copy-start(f32[2,16,64,512]{3,2,1,0:T(8,128)S(1)} %fusion.34) | copy-start | bytes 12582916
  232.4 2.0 copy-start
  242.7 5.7 %copy-start.3 = (f32[2,16,64,512]{3,2,1,0:T(8,128)S(1)}, f32[2,16,64,512]{3,2,1,0:T(8,128)}, u32[]{:S(2)}) copy-start(f32[2,16,64,512]{3,2,1,0:T(8,128)} %copy-done.2) | copy-start | bytes 12582916
  242.7 5.7 %copy-start.14 = (f32[128]{0:T(128)S(1)}, f32[128]{0:T(128)}, u32[]{:S(2)}) copy-start(f32[128]{0:T(128)} %get-tuple-element.66) | copy-start | bytes 1540
  254.3 102.1 %collective-permute-start.4 = (f32[2,3,64,128]{3,2,1,0:T(8,128)S(1)}, f32[2,3,64,128]{3,2,1,0:T(8,128)S(1)}, u32[]{:S(2)}, u32[]{:S(2)}) collective-permute-start(f32[2,3,64,128]{3,2,1,0:T(8,128)S(1)} %get-tuple-element.75), channel_id=1, source_target_pairs={{0,16},{16,32},{32,48},{48,64},{64,80},{80,96},{96,112},{1,17},{17... | collective-permute-start | bytes 589832 | tf_op jit(solution)/shard_map/ppermute | solution.py:17
  257.5 99.0 %collective-permute-start.5 = (f32[2,3,64,128]{3,2,1,0:T(8,128)S(1)}, f32[2,3,64,128]{3,2,1,0:T(8,128)S(1)}, u32[]{:S(2)}, u32[]{:S(2)}) collective-permute-start(f32[2,3,64,128]{3,2,1,0:T(8,128)S(1)} %get-tuple-element.76), channel_id=1, source_target_pairs={{16,0},{32,16},{48,32},{64,48},{80,64},{96,80},{112,96},{17,1},{33... | collective-permute-start | bytes 589832 | tf_op jit(solution)/shard_map/ppermute | solution.py:20
  259.2 21.3 %copy-start.11 = (f32[128]{0:T(128)S(1)}, f32[128]{0:T(128)}, u32[]{:S(2)}) copy-start(f32[128]{0:T(128)} %get-tuple-element.69) | copy-start | bytes 1540
  356.5 51.4 %collective-permute-start.6 = (f32[2,22,3,128]{3,2,1,0:T(4,128)S(1)}, f32[2,22,3,128]{3,2,1,0:T(4,128)S(1)}, u32[]{:S(2)}, u32[]{:S(2)}) collective-permute-start(f32[2,22,3,128]{3,2,1,0:T(4,128)S(1)} %get-tuple-element.71), channel_id=1, source_target_pairs={{0,1},{1,2},{2,3},{3,4},{4,5},{5,6},{6,7},{7,8},{8,9},{9,10},{10,1... | collective-permute-start | bytes 202760 | tf_op jit(solution)/shard_map/ppermute | solution.py:17
  358.9 48.9 %collective-permute-start.7 = (f32[2,22,3,128]{3,2,1,0:T(4,128)S(1)}, f32[2,22,3,128]{3,2,1,0:T(4,128)S(1)}, u32[]{:S(2)}, u32[]{:S(2)}) collective-permute-start(f32[2,22,3,128]{3,2,1,0:T(4,128)S(1)} %get-tuple-element.72), channel_id=1, source_target_pairs={{1,0},{2,1},{3,2},{4,3},{5,4},{6,5},{7,6},{8,7},{9,8},{10,9},{11,1... | collective-permute-start | bytes 202760 | tf_op jit(solution)/shard_map/ppermute | solution.py:20
  409.8 1.1 copy-start.17
  (3 other events, 2.2 us)
Sparse Core Ops, SparseCore 0:
  259.3 145.9 all-reduce.19
where the time goes:
time: 432 us; the launch traced here: 426 us
  blocking collectives  245 us (57%)
  matrix products  67.6 us (16%)
  waiting for transfers between devices  44.3 us (10%)
  local copies, waits for them, and re-layouts  23.5 us (5%)
  starting transfers between devices  22 us (5%)
  between operations  18.1 us (4%)
  other arithmetic  5.48 us (1%)
    unnamed x2, blocking collectives  135 us
    unnamed x2, waiting for transfers between devices  44.3 us
    all_gather x1, blocking collectives, per_device(): lax.all_gather(w_in, ('row', 'col'), axis=1, tiled=True)  38.5 us
    all_gather x1, blocking collectives, per_device(): lax.all_gather(w_out, ('row', 'col'), axis=0, tiled=True)  37.6 us
    all_gather x1, blocking collectives, per_device(): lax.all_gather(conv_kernel, ('row', 'col'), axis=2, tiled=True)  33.9 us
    conv_general_dilated x3, matrix products, depthwise(): lax.conv_general_dilated(field, kernel[:, :, None, :], (1, 1), 'VALID', d...  32.7 us
    unnamed x65, local copies, waits for them, and re-layouts  16.8 us
    ppermute x4, starting transfers between devices, extended(): lax.ppermute(lax.slice_in_dim(block, block.shape[dim] - width, None, axis...  14.4 us
  transfers between devices with their start and end apart: 9, of which 1 were waited for; matrix products, arithmetic and copies ran while one was open for 8% of the time, Pallas kernels for 0%

commit v1 on v0

--- a/solution.py
+++ b/solution.py
@@ -7,6 +7,13 @@
 norm_eps = 1e-06
 inverse_root_two = 0.7071067811865476
 inverse_root_twopi = 0.3989422804014327
+
+
+def exchange_gather(x, axis, d):
+    n_dev = lax.axis_size(axis)
+    blocks = jnp.stack([x for _ in range(n_dev)])
+    blocks = lax.all_to_all(blocks, axis, split_axis=0, concat_axis=0)
+    return jnp.concatenate(blocks, axis=d)
 
 
 def extended(block, sides, width):
@@ -101,7 +108,7 @@
         lax.all_gather(conv_bias, ("row", "col"), axis=0, tiled=True),
         lax.all_gather(norm_gain, ("row", "col"), axis=0, tiled=True),
         lax.all_gather(norm_shift, ("row", "col"), axis=0, tiled=True),
-        lax.all_gather(w_in, ("row", "col"), axis=1, tiled=True),
+        exchange_gather(w_in, ("row", "col"), 1),
         lax.all_gather(in_bias, ("row", "col"), axis=0, tiled=True),
         lax.all_gather(w_out, ("row", "col"), axis=0, tiled=True),
         lax.all_gather(out_bias, ("row", "col"), axis=0, tiled=True),

time: 432 us -> 409 us (0.947)
  blocking collectives: 245 us -> 212 us
  starting transfers between devices: 22 us -> 30.4 us
    all_gather x1 -> x0, blocking collectives: 38.5 us -> none  [per_device(): lax.all_gather(w_in, ('row', 'col'), axis=1, tiled=True)]
    all_to_all x0 -> x1, starting transfers between devices: none -> 7.68 us  [exchange_gather(): blocks = lax.all_to_all(blocks, axis, split_axis=0, concat_axis=0)]
    all_gather x1, blocking collectives: 33.9 us -> 40.9 us  [per_device(): lax.all_gather(conv_kernel, ('row', 'col'), axis=2, tiled=True)]
  transfers between devices with their start and end apart: 9 -> 10, of which waited for: 1 -> 1; matrix products, arithmetic and copies ran while one was open for 8% -> 11% of each run, Pallas kernels for 0% -> 0%
where the time goes in v1:
time: 409 us; the launch traced here: 403 us
  blocking collectives  212 us (52%)
  matrix products  67.6 us (17%)
  waiting for transfers between devices  44.7 us (11%)
  starting transfers between devices  30.4 us (7%)
  local copies, waits for them, and re-layouts  24.9 us (6%)
  between operations  18.1 us (4%)
  other arithmetic  5.48 us (1%)
    unnamed x2, blocking collectives  134 us
    unnamed x2, waiting for transfers between devices  44.7 us
    all_gather x1, blocking collectives, per_device(): lax.all_gather(conv_kernel, ('row', 'col'), axis=2, tiled=True)  40.9 us
    all_gather x1, blocking collectives, per_device(): lax.all_gather(w_out, ('row', 'col'), axis=0, tiled=True)  37 us
    conv_general_dilated x3, matrix products, depthwise(): lax.conv_general_dilated(field, kernel[:, :, None, :], (1, 1), 'VALID', d...  32.7 us
    unnamed x65, local copies, waits for them, and re-layouts  16.8 us
    ppermute x4, starting transfers between devices, extended(): lax.ppermute(lax.slice_in_dim(block, block.shape[dim] - width, None, axis...  15.2 us
    dot_general x1, matrix products, mixing_back(): win_grad = jnp.einsum('bhwc,bhwk->ck', lin, d_act, precision=highest)  8.25 us
  transfers between devices with their start and end apart: 10, of which 1 were waited for; matrix products, arithmetic and copies ran while one was open for 11% of the time, Pallas kernels for 0%

profile of v1, /device:TPU:1, one launch (start us, length us, event | category | flops | bytes accessed | tf_op | source)
XLA Modules:
  0.0 402.9 jit_solution(15342003411575332542)
XLA Ops:
  9.2 7.1 %collective-permute-start = (f32[2,3,64,128]{3,0,2,1:T(2,128)}, f32[2,3,64,128]{3,0,2,1:T(2,128)}, u32[]{:S(2)}, u32[]{:S(2)}) collective-permute-start(f32[2,3,64,128]{3,0,2,1:T(2,128)} %copy.137), channel_id=1, source_target_pairs={{0,16},{16,32},{32,48},{48,64},{64,80},{80,96},{96,112},{1,17},{17... | collective-permute-start | bytes 589832 | tf_op jit(solution)/shard_map/ppermute | solution.py:24
  17.7 7.7 %all-to-all-start = ((f32[128,128,4]{1,2,0:T(4,128)}), f32[128,128,4]{1,2,0:T(4,128)S(1)}, u32[]{:S(2)}, u32[]{:S(2)}) async-start(f32[128,128,4]{1,2,0:T(4,128)} %stack.2), calls=%async_computation | async-start | bytes 524288 | tf_op jit(solution)/shard_map/all_to_all | solution.py:15
  31.5 40.9 %all_gather.24 = f32[7,7,128]{1,0,2:T(8,128)S(1)} all-gather(f32[7,7,1]{1,0,2:T(8,128)S(1)} %copy.78), channel_id=1, replica_groups=mesh['row'=8,'col'=16] {'row','col'}, dimensions={2}, use_global_device_ids=true | all-gather | bytes 25284 | tf_op jit(solution)/shard_map/all_gather | solution.py:107
  74.6 62.8 %all-reduce.16 = (f32[128]{0:T(128)S(1)}, f32[128]{0:T(128)S(1)}, f32[128]{0:T(128)}, f32[512]{0:T(512)}, f32[128]{0:T(128)S(1)}, /*index=5*/f32[128]{0:T(128)}) all-reduce(f32[128]{0:T(128)S(1)} %dynamic-update-slice.3, f32[128]{0:T(128)S(1)} %dynamic-update-slice.2, ...), channel_id=1, replica_groups=mesh['row'=8,'col'=16] {'row','col'}, use_global_device_ids=true, to_apply=%add.3 | all-reduce | flops 1152 | bytes 9216
  140.6 3.0 collective-permute-start.2
  143.6 1.9 collective-permute-start.3
  145.5 37.0 %all-gather = f32[128,4,128]{2,1,0:T(4,128)S(1)} all-gather(f32[1,4,128]{2,1,0:T(4,128)S(1)} %bitcast.96), channel_id=1, replica_groups=mesh['row'=8,'col'=16] {'row','col'}, dimensions={0}, use_global_device_ids=true | all-gather | bytes 264192 | tf_op jit(solution)/shard_map/all_gather | solution.py:113
  184.7 5.9 %fusion.56 = (f32[16,16,9]{1,2,0:T(8,128)S(1)}, f32[16,16,9,128]{3,1,2,0:T(8,128)S(1)}) fusion(f32[128]{0:T(128)S(1)} %copy-done.15, f32[7,7,1,128]{3,2,1,0:T(1,128)S(1)} %copy-done.7, f32[22,2,7,6,128]{4,2,1,3,0:T(8,128)S(1)} %slice.41, f32[22,2,8,9,128]{4,2,1,3,0:T(8,128)S(1)} %copy.77, pred[16,9]{0,1:T(8,128)(4,1)S(1)} %copy-done.16), kind=kOutput, calls=%fused_computation.87 | convolution fusion | flops 176318208 | bytes 3782800 | tf_op jit(solution)/shard_map/conv_general_dilated | solution.py:33
  192.2 3.6 fusion.34
  195.8 8.0 %fusion.30 = f32[512,128]{1,0:T(8,128)} fusion(f32[2,16,64,512]{3,2,1,0:T(8,128)S(1)} %fusion.34, f32[512]{0:T(512)S(1)} %copy-done.12, f32[2,16,64,128]{3,2,1,0:T(8,128)S(1)} %copy-done.1, f32[128]{0:T(128)S(1)} %copy-done.10), kind=kOutput, calls=%fused_computation.33 | convolution fusion | flops 1616183296 | bytes 5507584 | tf_op jit(solution)/shard_map/bhwk,bhwc->kc/dot_general | solution.py:87
  203.9 5.2 %fusion.57 = (f32[512]{0:T(512)S(1)}, f32[2,16,64,512]{3,2,1,0:T(8,128)S(1)}) fusion(f32[2,16,64,512]{3,2,1,0:T(8,128)S(1)} %fusion.34, f32[512]{0:T(512)S(1)} %copy-done.12, f32[512,128,1,1]{1,0,3,2:T(8,128)S(1)} %bitcast.94, f32[2,16,64,128]{3,2,1,0:T(8,128)S(1)} %copy-done.1, f32[128]{0:T(128)S(1)} %copy-done.10), kind=kOutput, calls=%fused_computation.88 | convolution fusion | flops 1622408704 | bytes 9703936 | tf_op jit(solution)/shard_map/bhwc,kc->bhwk/dot_general | solution.py:70
  209.1 2.0 copy-done
  211.0 8.3 %fusion.28 = f32[128,512]{0,1:T(8,128)} fusion(f32[2,16,64,512]{3,2,1,0:T(8,128)S(1)} %get-tuple-element.83, f32[128]{0:T(128)S(1)} %get-tuple-element.61, f32[128]{0:T(128)S(1)} %get-tuple-element.62, f32[16,2,64,128]{3,0,2,1:T(8,128)S(1)} %slice.42, f32[2,16,64]{2,1,0:T(8,128)S(1)} %add_rsqrt_fusion, f32[2,16,64]{2,1,0:T(8,128)S(1)} %copy.84), kind=kOutput, calls=%fused_computation.31 | convolution fusion | flops 1611726848 | bytes 5522432 | tf_op jit(solution)/shard_map/bhwc,bhwk->ck/dot_general | solution.py:85
  219.3 5.7 %multiply_reduce_fusion = (f32[128]{0:T(128)S(1)}, f32[2,16,64]{2,1,0:T(8,128)S(1)}, f32[2,16,64]{2,1,0:T(8,128)S(1)}, f32[128]{0:T(128)S(1)}, f32[2,16,64,128]{3,2,1,0:T(8,128)S(1)}) fusion(f32[2,16,64]{2,1,0:T(8,128)S(1)} %add_rsqrt_fusion, f32[2,16,64]{2,1,0:T(8,128)S(1)} %copy.84, f32[16,2,64,128]{3,0,2,1:T(8,128)S(1)} %slice.42, ...), kind=kOutput, calls=%fused_computation.40 | convolution fusion | flops 1612967680 | bytes 6587904 | tf_op jit(solution)/shard_map/bhwk,ck->bhwc/dot_general | solution.py:76
  225.0 4.1 %fusion.27 = f32[128]{0:T(128)S(1)} fusion(f32[2,16,64,128]{3,2,1,0:T(8,128)S(1)} %copy-done.1, f32[512,128,1,1]{1,0,3,2:T(8,128)S(1)} %bitcast.95, f32[2,16,64,512]{3,2,1,0:T(8,128)S(1)} %copy-done.3, f32[512]{0:T(512)S(1)} %copy-done.12, f32[128]{0:T(128)S(1)} %copy-done.14), kind=kOutput, calls=%fused_computation.29 | convolution fusion | flops 1616641920 | bytes 5508096 | tf_op jit(solution)/shard_map/bhwk,kc->bhwc/dot_general | solution.py:68
  229.1 1.8 fusion.52
  231.0 3.1 collective-permute-start.4
  234.1 1.7 collective-permute-start.5
  235.9 21.3 %convolution_multiply_fusion = f32[7,7,1,128]{3,2,1,0:T(1,128)S(1)} fusion(f32[2,16,64,128]{3,2,1,0:T(8,128)S(1)} %get-tuple-element.70, f32[2,22,3,128]{3,0,2,1:T(2,128)} %copy-done.6, f32[2,22,64,128]{3,0,2,1:T(2,128)} %copy-done.4, f32[2,22,3,128]{3,0,2,1:T(2,128)S(1)} %collective-permute-done.2), kind=kOutput, calls=%fused_computation.34 | convolution fusion | flops 154935424 | bytes 2650624 | tf_op jit(solution)/shard_map/transpose(jvp())/conv_general_dilated | solution.py:33
  257.5 71.0 %all-reduce.15 = (f32[7,7,128]{1,0,2:T(8,128)}, f32[128]{0:T(128)S(1)}, f32[128]{0:T(128)S(1)}, f32[128]{0:T(128)S(1)}, f32[512]{0:T(512)S(1)}, /*index=5*/f32[128]{0:T(128)S(1)}, f32[128]{0:T(128)S(1)}) all-reduce(f32[7,7,128]{1,0,2:T(8,128)S(1)} %bitcast.92, ...), channel_id=2, replica_groups=mesh['row'=8,'col'=16] {'row','col'}, use_global_device_ids=true, to_apply=%region_4.0.clone | all-reduce | flops 7424 | bytes 59392
  333.3 2.0 collective-permute-start.6
  335.3 2.6 collective-permute-start.7
  337.8 44.7 %all-reduce.20.cloned.1.call-done = (f32[128,512]{0,1:T(8,128)}, f32[512,128]{1,0:T(8,128)}) async-done(((f32[128,512]{0,1:T(8,128)}, f32[512,128]{1,0:T(8,128)}), (f32[128,512]{0,1:T(8,128)}, f32[512,128]{1,0:T(8,128)})) %all-reduce.20.cloned.1.call-update) | async-done | bytes 524304
  388.0 5.4 %fusion.18 = f32[16,16,9,128]{3,1,2,0:T(8,128)S(1)} fusion(f32[7,7,1,128]{3,2,1,0:T(1,128)S(1)} %copy.89, f32[22,2,8,15,128]{4,1,3,2,0:T(2,128)S(1)} %fusion.5, pred[16,9]{0,1:T(8,128)(4,1)S(1)} %copy-done.17), kind=kOutput, calls=%fused_computation.26 | convolution fusion | flops 173703168 | bytes 3908240 | tf_op jit(solution)/shard_map/conv_general_dilated | solution.py:33
  (111 shorter events, 27.9 us)
Async XLA Ops:
  7.2 67.2 %copy-start.13 = (f32[4]{0:T(128)S(1)}, f32[4]{0:T(128)}, u32[]{:S(2)}) copy-start(f32[4]{0:T(128)} %param.18) | copy-start | bytes 52
  7.2 130.2 %copy-start.1 = (f32[2,16,64,128]{3,2,1,0:T(8,128)S(1)}, f32[2,16,64,128]{3,2,1,0:T(8,128)}, u32[]{:S(2)}) copy-start(f32[2,16,64,128]{3,2,1,0:T(8,128)} %param.12) | copy-start | bytes 3145732
  9.2 129.5 %copy-start.5 = (f32[2,16,64,128]{3,2,1,0:T(8,128)S(1)}, f32[2,16,64,128]{3,2,1,0:T(8,128)}, u32[]{:S(2)}) copy-start(f32[2,16,64,128]{3,2,1,0:T(8,128)} %param.11) | copy-start | bytes 3145732
  9.2 128.5 %collective-permute-start = (f32[2,3,64,128]{3,0,2,1:T(2,128)}, f32[2,3,64,128]{3,0,2,1:T(2,128)}, u32[]{:S(2)}, u32[]{:S(2)}) collective-permute-start(f32[2,3,64,128]{3,0,2,1:T(2,128)} %copy.137), channel_id=1, source_target_pairs={{0,16},{16,32},{32,48},{48,64},{64,80},{80,96},{96,112},{1,17},{17... | collective-permute-start | bytes 589832 | tf_op jit(solution)/shard_map/ppermute | solution.py:24
  17.7 174.4 %all-to-all-start = ((f32[128,128,4]{1,2,0:T(4,128)}), f32[128,128,4]{1,2,0:T(4,128)S(1)}, u32[]{:S(2)}, u32[]{:S(2)}) async-start(f32[128,128,4]{1,2,0:T(4,128)} %stack.2), calls=%async_computation | async-start | bytes 524288 | tf_op jit(solution)/shard_map/all_to_all | solution.py:15
  25.4 357.1 %all-reduce.20.cloned.1.call-start = ((), (), s32[]{:S(2)}) async-start(), calls=%async_computation.1 | async-start | bytes 1048576
  26.3 113.3 %collective-permute-start.1 = (f32[2,3,64,128]{3,0,2,1:T(2,128)}, f32[2,3,64,128]{3,0,2,1:T(2,128)}, u32[]{:S(2)}, u32[]{:S(2)}) collective-permute-start(f32[2,3,64,128]{3,0,2,1:T(2,128)} %copy.138), channel_id=1, source_target_pairs={{16,0},{32,16},{48,32},{64,48},{80,64},{96,80},{112,96},{17,1},{33... | collective-permute-start | bytes 589832 | tf_op jit(solution)/shard_map/ppermute | solution.py:27
  72.8 72.7 %copy-start.8 = (f32[4,128]{1,0:T(4,128)S(1)}, f32[4,128]{1,0:T(4,128)}, u32[]{:S(2)}) copy-start(f32[4,128]{1,0:T(4,128)} %param.19) | copy-start | bytes 6148
  137.4 8.1 %copy-start.9 = (f32[128]{0:T(128)}, f32[128]{0:T(128)S(1)}, u32[]{:S(2)}) copy-start(f32[128]{0:T(128)S(1)} %get-tuple-element.65) | copy-start | bytes 1540
  140.5 43.4 %copy-start.4 = (f32[2,22,64,128]{3,0,2,1:T(2,128)}, f32[2,22,64,128]{3,0,2,1:T(2,128)S(1)}, u32[]{:S(2)}) copy-start(f32[2,22,64,128]{3,0,2,1:T(2,128)S(1)} %constant_dynamic-update-slice_fusion) | copy-start | bytes 4325380
  140.6 42.0 %collective-permute-start.2 = (f32[2,22,3,128]{3,0,2,1:T(2,128)S(1)}, f32[2,22,3,128]{3,0,2,1:T(2,128)S(1)}, u32[]{:S(2)}, u32[]{:S(2)}) collective-permute-start(f32[2,22,3,128]{3,0,2,1:T(2,128)S(1)} %get-tuple-element.73), channel_id=1, source_target_pairs={{0,1},{1,2},{2,3},{3,4},{4,5},{5,6},{6,7},{7,8},{8,9},{9,10},{10,1... | collective-permute-start | bytes 202760 | tf_op jit(solution)/shard_map/ppermute | solution.py:24
  143.6 39.0 %collective-permute-start.3 = (f32[2,22,3,128]{3,0,2,1:T(2,128)S(1)}, f32[2,22,3,128]{3,0,2,1:T(2,128)S(1)}, u32[]{:S(2)}, u32[]{:S(2)}) collective-permute-start(f32[2,22,3,128]{3,0,2,1:T(2,128)S(1)} %get-tuple-element.74), channel_id=1, source_target_pairs={{1,0},{2,1},{3,2},{4,3},{5,4},{6,5},{7,6},{8,7},{9,8},{10,9},{11,1... | collective-permute-start | bytes 202760 | tf_op jit(solution)/shard_map/ppermute | solution.py:27
  182.6 1.6 copy-start.6
  192.1 3.7 copy-start.10
  192.1 3.7 copy-start.12
  195.8 8.1 %copy-start.2 = (f32[2,16,64,512]{3,2,1,0:T(8,128)}, f32[2,16,64,512]{3,2,1,0:T(8,128)S(1)}, u32[]{:S(2)}) copy-start(f32[2,16,64,512]{3,2,1,0:T(8,128)S(1)} %fusion.34) | copy-start | bytes 12582916
  209.0 2.0 copy-start
  219.3 5.7 %copy-start.3 = (f32[2,16,64,512]{3,2,1,0:T(8,128)S(1)}, f32[2,16,64,512]{3,2,1,0:T(8,128)}, u32[]{:S(2)}) copy-start(f32[2,16,64,512]{3,2,1,0:T(8,128)} %copy-done.2) | copy-start | bytes 12582916
  219.3 5.7 %copy-start.14 = (f32[128]{0:T(128)S(1)}, f32[128]{0:T(128)}, u32[]{:S(2)}) copy-start(f32[128]{0:T(128)} %get-tuple-element.66) | copy-start | bytes 1540
  231.0 102.3 %collective-permute-start.4 = (f32[2,3,64,128]{3,2,1,0:T(8,128)S(1)}, f32[2,3,64,128]{3,2,1,0:T(8,128)S(1)}, u32[]{:S(2)}, u32[]{:S(2)}) collective-permute-start(f32[2,3,64,128]{3,2,1,0:T(8,128)S(1)} %get-tuple-element.75), channel_id=1, source_target_pairs={{0,16},{16,32},{32,48},{48,64},{64,80},{80,96},{96,112},{1,17},{17... | collective-permute-start | bytes 589832 | tf_op jit(solution)/shard_map/ppermute | solution.py:24
  234.1 99.1 %collective-permute-start.5 = (f32[2,3,64,128]{3,2,1,0:T(8,128)S(1)}, f32[2,3,64,128]{3,2,1,0:T(8,128)S(1)}, u32[]{:S(2)}, u32[]{:S(2)}) collective-permute-start(f32[2,3,64,128]{3,2,1,0:T(8,128)S(1)} %get-tuple-element.76), channel_id=1, source_target_pairs={{16,0},{32,16},{48,32},{64,48},{80,64},{96,80},{112,96},{17,1},{33... | collective-permute-start | bytes 589832 | tf_op jit(solution)/shard_map/ppermute | solution.py:27
  235.9 21.3 %copy-start.11 = (f32[128]{0:T(128)S(1)}, f32[128]{0:T(128)}, u32[]{:S(2)}) copy-start(f32[128]{0:T(128)} %get-tuple-element.69) | copy-start | bytes 1540
  333.3 51.7 %collective-permute-start.6 = (f32[2,22,3,128]{3,2,1,0:T(4,128)S(1)}, f32[2,22,3,128]{3,2,1,0:T(4,128)S(1)}, u32[]{:S(2)}, u32[]{:S(2)}) collective-permute-start(f32[2,22,3,128]{3,2,1,0:T(4,128)S(1)} %get-tuple-element.71), channel_id=1, source_target_pairs={{0,1},{1,2},{2,3},{3,4},{4,5},{5,6},{6,7},{7,8},{8,9},{9,10},{10,1... | collective-permute-start | bytes 202760 | tf_op jit(solution)/shard_map/ppermute | solution.py:24
  335.3 49.8 %collective-permute-start.7 = (f32[2,22,3,128]{3,2,1,0:T(4,128)S(1)}, f32[2,22,3,128]{3,2,1,0:T(4,128)S(1)}, u32[]{:S(2)}, u32[]{:S(2)}) collective-permute-start(f32[2,22,3,128]{3,2,1,0:T(4,128)S(1)} %get-tuple-element.72), channel_id=1, source_target_pairs={{1,0},{2,1},{3,2},{4,3},{5,4},{6,5},{7,6},{8,7},{9,8},{10,9},{11,1... | collective-permute-start | bytes 202760 | tf_op jit(solution)/shard_map/ppermute | solution.py:27
  (4 other events, 3.3 us)
Sparse Core Ops, SparseCore 0:
  236.0 146.4 all-reduce.19
